TPU v7x, 32 devices: a whole 2x2x4 slice. The times are simulated.
32 devices in a mesh: dp: 4 (over z), ctx: 2 (over x), hidden: 4 (over y, core).
Axes of the slice: x: 2, y: 2, z: 4, core: 2. Of those that a mesh axis runs over, the one named last changes fastest.
Arguments:
- activations: bfloat16 [4, 1024, 53248], P('dp', 'ctx', 'hidden'), may hold values from -6 to 6
- out_grads: bfloat16 [4, 1024, 16384], P('dp', 'ctx', 'hidden'), may hold values from -0.1875 to 0.1875
- input_basis: bfloat16 [53248, 512], P('hidden', ('dp', 'ctx')), may hold values from -0.02734375 to 0.02734375
- output_basis: bfloat16 [16384, 512], P('hidden', ('dp', 'ctx')), may hold values from -0.046875 to 0.046875
- rotation: bfloat16 [512, 512], P('ctx'), may hold values from -0.25 to 0.25
Outputs:
- logged: float32 [4, 512, 512], P('dp', 'ctx', 'hidden')
All inputs are finite; a program needn't handle non-finite values.
Results may differ from a plain program's by a relative error of at most 0.0049.
Values may be sent and summed in bfloat16 or wider, within the bound.
A program may use at most 64 MiB of HBM per device.

v0:
```python
import jax
import jax.numpy as jnp
from jax import lax
from jax.sharding import PartitionSpec as P


def outer_sum(left, right):
    return lax.dot_general(
        left, right, (((0,), (0,)), ((), ())), preferred_element_type=jnp.float32
    )


def local(activations, out_grads, input_basis, output_basis, rotation):
    tokens = activations.reshape(-1, activations.shape[-1])
    grad_rows = out_grads.reshape(-1, out_grads.shape[-1])
    in_part = jnp.dot(
        tokens,
        lax.all_gather(input_basis, ("dp", "ctx"), axis=1, tiled=True),
        preferred_element_type=jnp.float32,
    )
    out_part = jnp.dot(
        grad_rows,
        lax.all_gather(output_basis, ("dp", "ctx"), axis=1, tiled=True),
        preferred_element_type=jnp.float32,
    )
    in_cols = lax.psum_scatter(in_part, "hidden", scatter_dimension=1, tiled=True).astype(
        jnp.bfloat16
    )
    out_side = lax.psum(out_part, "hidden")
    out_side = out_side.astype(jnp.bfloat16)
    total = lax.psum(outer_sum(out_side, in_cols), "ctx")
    lowrank = total.astype(jnp.bfloat16)
    logged = jnp.dot(rotation, lowrank, preferred_element_type=jnp.float32)
    return logged.reshape(1, logged.shape[0], logged.shape[1])


def solution(mesh):
    return jax.shard_map(
        local,
        mesh=mesh,
        in_specs=(
            P("dp", "ctx", "hidden"),
            P("dp", "ctx", "hidden"),
            P("hidden", ("dp", "ctx")),
            P("hidden", ("dp", "ctx")),
            P("ctx", None),
        ),
        out_specs=P("dp", "ctx", "hidden"),
        check_vma=False,
    )
```

profile of v0, /device:TPU:0, one launch (start us, length us, event | category | flops | bytes accessed | tf_op | source)
XLA Modules:
  0.0 329.6 jit_solution(16970726115371257310)
XLA Ops:
  6.5 0.0 copy-start
  6.5 0.0 all-gather.5.cloned.1.call-start
  6.5 0.7 all-gather.5.cloned.1.call-update
  7.3 0.0 all-gather.3.cloned.1.call-start
  7.3 0.7 all-gather.3.cloned.1.call-update
  8.0 0.0 reduce-scatter.2.cloned.1.call-start
  8.1 193.1 %all-gather.5.cloned.1.call-done = bf16[13312,512]{0,1:T(8,128)(2,1)} async-done(((bf16[13312,64]{0,1:T(8,128)(2,1)}), bf16[13312,512]{0,1:T(8,128)(2,1)}) %all-gather.5.cloned.1.call-update) | async-done | bytes 13631504 | tf_op jit(solution)/shard_map/all_gather | solution.py:18
  201.2 15.1 %fusion = f32[512,512]{1,0:T(8,128)} fusion(bf16[13312,512]{0,1:T(8,128)(2,1)} %all-gather.5.cloned.1.call-done, bf16[1,512,13312]{2,1,0:T(8,128)(2,1)} %param.5), kind=kOutput, calls=%fused_computation | convolution fusion | flops 6979321856 | bytes 28311552 | tf_op jit(solution)/shard_map/dot_general | solution.py:16
  216.3 0.0 reduce-scatter.2.cloned.1.call-update
  216.3 58.0 %all-gather.3.cloned.1.call-done = bf16[4096,512]{0,1:T(8,128)(2,1)} async-done(((bf16[4096,64]{0,1:T(8,128)(2,1)}), bf16[4096,512]{0,1:T(8,128)(2,1)}) %all-gather.3.cloned.1.call-update) | async-done | bytes 4194320 | tf_op jit(solution)/shard_map/all_gather | solution.py:23
  274.3 5.8 %fusion.2 = f32[512,512]{1,0:T(8,128)S(1)} fusion(bf16[4096,512]{0,1:T(8,128)(2,1)} %all-gather.3.cloned.1.call-done, bf16[1,512,4096]{2,1,0:T(8,128)(2,1)} %param.6), kind=kOutput, calls=%fused_computation.2 | convolution fusion | flops 2147483648 | bytes 9437184 | tf_op jit(solution)/shard_map/dot_general | solution.py:21
  280.1 28.4 %all-reduce.2 = bf16[512,512]{1,0:T(8,128)(2,1)S(1)} all-reduce(f32[512,512]{1,0:T(8,128)S(1)} %fusion.2), channel_id=1, replica_groups=mesh['dp'=4,'ctx'=2,'hidden'=4] {'hidden'}, use_global_device_ids=true, to_apply=%region_0.0 | all-reduce | flops 262144 | bytes 1572864 | tf_op jit(solution)/shard_map/psum | solution.py:29
  308.5 0.0 reduce-scatter.2.cloned.1.call-done
  308.6 1.3 fusion.4
  309.8 12.2 %all-reduce.3 = bf16[512,128]{1,0:T(8,128)(2,1)S(1)} all-reduce(f32[512,128]{1,0:T(8,128)S(1)} %fusion.4), channel_id=1, replica_groups=mesh['dp'=4,'ctx'=2,'hidden'=4] {'ctx'}, use_global_device_ids=true, to_apply=%region_2.0 | all-reduce | flops 65536 | bytes 393216 | tf_op jit(solution)/shard_map/psum | solution.py:31
  322.1 0.0 copy-done
  322.1 0.2 convolution_bitcast_fusion
  322.3 0.8 copy.6
Async XLA Ops:
  6.5 315.5 %copy-start = (bf16[256,512]{1,0:T(8,128)(2,1)S(1)}, bf16[256,512]{1,0:T(8,128)(2,1)}, u32[]{:S(2)}) copy-start(bf16[256,512]{1,0:T(8,128)(2,1)} %param.9) | copy-start | bytes 786436
  6.5 194.6 %all-gather.5.cloned.1.call-start = ((), (), s32[]{:S(2)}) async-start(), calls=%async_computation.2 | async-start | bytes 15335424 | tf_op jit(solution)/shard_map/all_gather | solution.py:18
  7.3 267.0 %all-gather.3.cloned.1.call-start = ((), (), s32[]{:S(2)}) async-start(), calls=%async_computation.1 | async-start | bytes 4718592 | tf_op jit(solution)/shard_map/all_gather | solution.py:23
  8.0 300.5 %reduce-scatter.2.cloned.1.call-start = ((), (), s32[]{:S(2)}) async-start(), calls=%async_computation.3 | async-start | bytes 1310720 | tf_op jit(solution)/shard_map/reduce_scatter | solution.py:26
Sparse Core Ops, SparseCore 0:
  9.5 191.5 all-gather.4
  203.3 70.9 all-gather.2
  276.8 26.8 reduce-scatter.1
where the time goes:
time: 330 us
  waiting for transfers between devices  253 us (77%)
  blocking collectives  40.6 us (12%)
  matrix products  22.5 us (7%)
  between operations  13.2 us (4%)
    all_gather x1, waiting for transfers between devices, local(): lax.all_gather(input_basis, ('dp', 'ctx'), axis=1, tiled=True)  193 us
    all_gather x1, waiting for transfers between devices, local(): lax.all_gather(output_basis, ('dp', 'ctx'), axis=1, tiled=True)  58 us
    psum x1, blocking collectives, local(): out_side = lax.psum(out_part, 'hidden')  28.4 us
    dot_general x1, matrix products, local(): jnp.dot(tokens, lax.all_gather(input_basis, ('dp', 'ctx'), axis=1, tiled=...  15.1 us
    psum x1, blocking collectives, local(): total = lax.psum(outer_sum(out_side, in_cols), 'ctx')  12.2 us
  transfers between devices with their start and end apart: 3, of which 2 were waited for; matrix products, arithmetic and copies ran while one was open for 6% of the time, Pallas kernels for 0%

commit v1 on v0

--- a/solution.py
+++ b/solution.py
@@ -26,7 +26,7 @@
     in_cols = lax.psum_scatter(in_part, "hidden", scatter_dimension=1, tiled=True).astype(
         jnp.bfloat16
     )
-    out_side = lax.psum(out_part, "hidden")
+    out_side = jnp.sum(lax.all_gather(out_part, "hidden"), axis=0)
     out_side = out_side.astype(jnp.bfloat16)
     total = lax.psum(outer_sum(out_side, in_cols), "ctx")
     lowrank = total.astype(jnp.bfloat16)

time: 330 us -> 356 us (1.079)
  waiting for transfers between devices: 253 us -> 304 us
  blocking collectives: 40.6 us -> 11.3 us
    psum x1 -> x0, blocking collectives: 28.4 us -> none  [local(): out_side = lax.psum(out_part, 'hidden')]
    reduce_scatter x1, waiting for transfers between devices: 0.02 us -> 24.5 us  [local(): lax.psum_scatter(in_part, 'hidden', scatter_dimension=1, tiled=True)]
    all_gather x1, waiting for transfers between devices: 58 us -> 76.9 us  [local(): lax.all_gather(output_basis, ('dp', 'ctx'), axis=1, tiled=True)]
    all_gather x0 -> x1, waiting for transfers between devices: none -> 18.7 us  [local(): out_side = jnp.sum(lax.all_gather(out_part, 'hidden'), axis=0)]
    all_gather x1, waiting for transfers between devices: 193 us -> 183 us  [local(): lax.all_gather(input_basis, ('dp', 'ctx'), axis=1, tiled=True)]
  transfers between devices with their start and end apart: 3 -> 4, of which waited for: 2 -> 4; matrix products, arithmetic and copies ran while one was open for 6% -> 7% of each run, Pallas kernels for 0% -> 0%
where the time goes in v1:
time: 356 us
  waiting for transfers between devices  304 us (85%)
  matrix products  23.9 us (7%)
  between operations  13.2 us (4%)
  blocking collectives  11.3 us (3%)
    all_gather x1, waiting for transfers between devices, local(): lax.all_gather(input_basis, ('dp', 'ctx'), axis=1, tiled=True)  183 us
    all_gather x1, waiting for transfers between devices, local(): lax.all_gather(output_basis, ('dp', 'ctx'), axis=1, tiled=True)  76.9 us
    reduce_scatter x1, waiting for transfers between devices, local(): lax.psum_scatter(in_part, 'hidden', scatter_dimension=1, tiled=True)  24.5 us
    all_gather x1, waiting for transfers between devices, local(): out_side = jnp.sum(lax.all_gather(out_part, 'hidden'), axis=0)  18.7 us
    dot_general x1, matrix products, local(): jnp.dot(tokens, lax.all_gather(input_basis, ('dp', 'ctx'), axis=1, tiled=...  15.5 us
    psum x1, blocking collectives, local(): total = lax.psum(outer_sum(out_side, in_cols), 'ctx')  11.3 us
  transfers between devices with their start and end apart: 4, of which 4 were waited for; matrix products, arithmetic and copies ran while one was open for 7% of the time, Pallas kernels for 0%

profile of v1, /device:TPU:0, one launch (start us, length us, event | category | flops | bytes accessed | tf_op | source)
XLA Modules:
  0.0 356.3 jit_solution(15177708152345942377)
XLA Ops:
  6.5 0.0 copy-start
  6.5 0.0 all-gather.5.cloned.1.call-start
  6.5 0.7 all-gather.5.cloned.1.call-update
  7.3 0.0 all-gather.7.cloned.1.call-start
  7.3 0.7 all-gather.7.cloned.1.call-update
  8.0 0.0 all-gather.9.cloned.1.call-start
  8.1 76.9 %all-gather.5.cloned.1.call-done = bf16[4096,512]{0,1:T(8,128)(2,1)} async-done(((bf16[4096,64]{0,1:T(8,128)(2,1)}), bf16[4096,512]{0,1:T(8,128)(2,1)}) %all-gather.5.cloned.1.call-update) | async-done | bytes 4194320 | tf_op jit(solution)/shard_map/all_gather | solution.py:23
  85.0 6.8 %fusion.2 = f32[512,512]{1,0:T(8,128)} fusion(bf16[4096,512]{0,1:T(8,128)(2,1)} %all-gather.5.cloned.1.call-done, bf16[1,512,4096]{2,1,0:T(8,128)(2,1)} %param.6), kind=kOutput, calls=%fused_computation.2 | convolution fusion | flops 2147483648 | bytes 9437184 | tf_op jit(solution)/shard_map/dot_general | solution.py:21
  91.8 0.0 all-gather.9.cloned.1.call-update
  91.9 0.0 reduce-scatter.2.cloned.1.call-start
  91.9 182.7 %all-gather.7.cloned.1.call-done = bf16[13312,512]{0,1:T(8,128)(2,1)} async-done(((bf16[13312,64]{0,1:T(8,128)(2,1)}), bf16[13312,512]{0,1:T(8,128)(2,1)}) %all-gather.7.cloned.1.call-update) | async-done | bytes 13631504 | tf_op jit(solution)/shard_map/all_gather | solution.py:18
  274.6 15.5 %fusion = f32[512,512]{1,0:T(8,128)} fusion(bf16[13312,512]{0,1:T(8,128)(2,1)} %all-gather.7.cloned.1.call-done, bf16[1,512,13312]{2,1,0:T(8,128)(2,1)} %param.5), kind=kOutput, calls=%fused_computation | convolution fusion | flops 6979321856 | bytes 28311552 | tf_op jit(solution)/shard_map/dot_general | solution.py:16
  290.2 0.0 reduce-scatter.2.cloned.1.call-update
  290.2 18.7 %all-gather.9.cloned.1.call-done = f32[2048,512]{1,0:T(8,128)} async-done(((f32[512,512]{1,0:T(8,128)}), f32[2048,512]{1,0:T(8,128)}) %all-gather.9.cloned.1.call-update) | async-done | bytes 4194320 | tf_op jit(solution)/shard_map/all_gather | solution.py:29
  308.9 2.7 reduce_sum.9
  311.6 24.5 %reduce-scatter.2.cloned.1.call-done = f32[512,128]{1,0:T(8,128)} async-done(((f32[512,512]{1,0:T(8,128)}), f32[512,128]{1,0:T(8,128)}) %reduce-scatter.2.cloned.1.call-update) | async-done | bytes 262160 | tf_op jit(solution)/shard_map/reduce_scatter | solution.py:26
  336.1 1.3 fusion.4
  337.4 11.3 %all-reduce.1 = bf16[512,128]{1,0:T(8,128)(2,1)S(1)} all-reduce(f32[512,128]{1,0:T(8,128)S(1)} %fusion.4), channel_id=1, replica_groups=mesh['dp'=4,'ctx'=2,'hidden'=4] {'ctx'}, use_global_device_ids=true, to_apply=%region_2.0 | all-reduce | flops 65536 | bytes 393216 | tf_op jit(solution)/shard_map/psum | solution.py:31
  348.7 0.0 copy-done
  348.8 0.2 convolution_bitcast_fusion
  349.0 0.8 copy.6
Async XLA Ops:
  6.5 342.2 %copy-start = (bf16[256,512]{1,0:T(8,128)(2,1)S(1)}, bf16[256,512]{1,0:T(8,128)(2,1)}, u32[]{:S(2)}) copy-start(bf16[256,512]{1,0:T(8,128)(2,1)} %param.9) | copy-start | bytes 786436
  6.5 78.5 %all-gather.5.cloned.1.call-start = ((), (), s32[]{:S(2)}) async-start(), calls=%async_computation.1 | async-start | bytes 4718592 | tf_op jit(solution)/shard_map/all_gather | solution.py:23
  7.3 267.4 %all-gather.7.cloned.1.call-start = ((), (), s32[]{:S(2)}) async-start(), calls=%async_computation.2 | async-start | bytes 15335424 | tf_op jit(solution)/shard_map/all_gather | solution.py:18
  8.0 300.9 %all-gather.9.cloned.1.call-start = ((), (), s32[]{:S(2)}) async-start(), calls=%async_computation.4 | async-start | bytes 5242880 | tf_op jit(solution)/shard_map/all_gather | solution.py:29
  91.9 244.3 %reduce-scatter.2.cloned.1.call-start = ((), (), s32[]{:S(2)}) async-start(), calls=%async_computation.3 | async-start | bytes 1310720 | tf_op jit(solution)/shard_map/reduce_scatter | solution.py:26
Sparse Core Ops, SparseCore 0:
  9.5 75.4 all-gather.4
  87.2 187.4 all-gather.6
  276.2 32.6 all-gather.8
  311.3 24.8 reduce-scatter.1

commit v2 on v0

--- a/solution.py
+++ b/solution.py
@@ -2,6 +2,18 @@
 import jax.numpy as jnp
 from jax import lax
 from jax.sharding import PartitionSpec as P
+
+
+def doubled_up(value, axis, dim):
+    ways, here, hop = (lax.axis_size(axis), lax.axis_index(axis), value.shape[dim])
+    line, have = (value, 1)
+    while have < ways:
+        line = jnp.concatenate(
+            [line, lax.ppermute(line, axis, [(d, (d - have) % ways) for d in range(ways)])],
+            axis=dim,
+        )
+        have = 2 * have
+    return jnp.roll(line, here * hop, axis=dim)
 
 
 def outer_sum(left, right):
@@ -19,9 +31,7 @@
         preferred_element_type=jnp.float32,
     )
     out_part = jnp.dot(
-        grad_rows,
-        lax.all_gather(output_basis, ("dp", "ctx"), axis=1, tiled=True),
-        preferred_element_type=jnp.float32,
+        grad_rows, doubled_up(output_basis, ("dp", "ctx"), 1), preferred_element_type=jnp.float32
     )
     in_cols = lax.psum_scatter(in_part, "hidden", scatter_dimension=1, tiled=True).astype(
         jnp.bfloat16

time: 330 us -> 378 us (1.15)
  waiting for transfers between devices: 253 us -> 278 us
  local copies, waits for them, and re-layouts: 0.76 us -> 11.5 us
  starting transfers between devices: 0.08 us -> 6.16 us
  other arithmetic: 0 us -> 3.89 us
    ppermute x0 -> x3, waiting for transfers between devices: none -> 256 us  [doubled_up(): lax.ppermute(line, axis, [(d, (d - have) % ways) for d in range(ways)])]
    all_gather x1, waiting for transfers between devices: 193 us -> 20.9 us  [local(): lax.all_gather(input_basis, ('dp', 'ctx'), axis=1, tiled=True)]
    all_gather x1 -> x0, waiting for transfers between devices: 58 us -> none  [local(): lax.all_gather(output_basis, ('dp', 'ctx'), axis=1, tiled=True)]
    unnamed x2 -> x15, local copies, waits for them, and re-layouts: 0.01 us -> 9.13 us
    ppermute x0 -> x3, starting transfers between devices: none -> 6.12 us  [doubled_up(): lax.ppermute(line, axis, [(d, (d - have) % ways) for d in range(ways)])]
    concatenate x0 -> x2, other arithmetic: none -> 3.89 us  [doubled_up(): jnp.concatenate([line, lax.ppermute(line, axis, [(d, (d - have) % ways) f...]
  transfers between devices with their start and end apart: 3 -> 5, of which waited for: 2 -> 4; matrix products, arithmetic and copies ran while one was open for 6% -> 5% of each run, Pallas kernels for 0% -> 0%
where the time goes in v2:
time: 378 us
  waiting for transfers between devices  278 us (74%)
  blocking collectives  42.3 us (11%)
  matrix products  22.4 us (6%)
  between operations  13.5 us (4%)
  local copies, waits for them, and re-layouts  11.5 us (3%)
  starting transfers between devices  6.16 us (2%)
  other arithmetic  3.89 us (1%)
    ppermute x3, waiting for transfers between devices, doubled_up(): lax.ppermute(line, axis, [(d, (d - have) % ways) for d in range(ways)])  256 us
    psum x1, blocking collectives, local(): out_side = lax.psum(out_part, 'hidden')  29.9 us
    all_gather x1, waiting for transfers between devices, local(): lax.all_gather(input_basis, ('dp', 'ctx'), axis=1, tiled=True)  20.9 us
    dot_general x1, matrix products, local(): jnp.dot(tokens, lax.all_gather(input_basis, ('dp', 'ctx'), axis=1, tiled=...  15.1 us
    psum x1, blocking collectives, local(): total = lax.psum(outer_sum(out_side, in_cols), 'ctx')  12.4 us
    unnamed x15, local copies, waits for them, and re-layouts  9.13 us
  transfers between devices with their start and end apart: 5, of which 4 were waited for; matrix products, arithmetic and copies ran while one was open for 5% of the time, Pallas kernels for 0%

profile of v2, /device:TPU:0, one launch (start us, length us, event | category | flops | bytes accessed | tf_op | source)
XLA Modules:
  0.0 377.7 jit_solution(6404543079348818538)
XLA Ops:
  6.5 0.7 all-gather.2.cloned.1.call-update
  7.3 6.1 %collective-permute-start = (bf16[4096,64]{0,1:T(8,128)(2,1)}, bf16[4096,64]{0,1:T(8,128)(2,1)S(1)}, u32[]{:S(2)}, u32[]{:S(2)}) collective-permute-start(bf16[4096,64]{0,1:T(8,128)(2,1)} %param.8), channel_id=1, source_target_pairs={{0,28},{4,0},{8,4},{12,8},{16,12},{20,16},{24,20},{28,24},{1,29},{... | collective-permute-start | bytes 1572872 | tf_op jit(solution)/shard_map/ppermute | solution.py:12
  13.4 15.4 %collective-permute-done = bf16[4096,64]{0,1:T(8,128)(2,1)S(1)} collective-permute-done((bf16[4096,64]{0,1:T(8,128)(2,1)}, bf16[4096,64]{0,1:T(8,128)(2,1)S(1)}, u32[]{:S(2)}, u32[]{:S(2)}) %collective-permute-start) | collective-permute-done | bytes 524320 | tf_op jit(solution)/shard_map/ppermute | solution.py:12
  28.8 1.3 pad_maximum_fusion.1
  30.1 0.1 collective-permute-start.1
  30.2 70.2 %collective-permute-done.1 = bf16[4096,128]{0,1:T(8,128)(2,1)S(1)} collective-permute-done((bf16[4096,128]{0,1:T(8,128)(2,1)S(1)}, bf16[4096,128]{0,1:T(8,128)(2,1)S(1)}, u32[]{:S(2)}, u32[]{:S(2)}) %collective-permute-start.1) | collective-permute-done | bytes 1048608 | tf_op jit(solution)/shard_map/ppermute | solution.py:12
  100.3 2.6 pad_maximum_fusion
  102.9 1.9 constant_dynamic-update-slice_fusion.7
  104.8 1.9 constant_dynamic-update-slice_fusion.6
  106.7 1.1 constant_dynamic-update-slice_fusion.5
  107.8 170.8 %collective-permute-done.2 = bf16[4096,256]{0,1:T(8,128)(2,1)S(1)} collective-permute-done((bf16[4096,256]{0,1:T(8,128)(2,1)}, bf16[4096,256]{0,1:T(8,128)(2,1)S(1)}, u32[]{:S(2)}, u32[]{:S(2)}) %collective-permute-start.2) | collective-permute-done | bytes 2097184 | tf_op jit(solution)/shard_map/ppermute | solution.py:12
  278.6 1.5 constant_dynamic-update-slice_fusion.4
  280.1 0.8 constant_dynamic-update-slice_fusion.3
  281.0 0.8 constant_dynamic-update-slice_fusion.2
  281.8 1.1 constant_dynamic-update-slice_fusion.1
  282.9 20.9 %all-gather.2.cloned.1.call-done = bf16[13312,512]{0,1:T(8,128)(2,1)} async-done(((bf16[13312,64]{0,1:T(8,128)(2,1)}), bf16[13312,512]{0,1:T(8,128)(2,1)}) %all-gather.2.cloned.1.call-update) | async-done | bytes 13631504 | tf_op jit(solution)/shard_map/all_gather | solution.py:30
  303.8 15.1 %fusion = f32[512,512]{1,0:T(8,128)} fusion(bf16[13312,512]{0,1:T(8,128)(2,1)} %all-gather.2.cloned.1.call-done, bf16[1,512,13312]{2,1,0:T(8,128)(2,1)} %param.5), kind=kOutput, calls=%fused_computation | convolution fusion | flops 6979321856 | bytes 28311552 | tf_op jit(solution)/shard_map/dot_general | solution.py:28
  318.9 1.6 constant_dynamic-update-slice_fusion
  320.5 5.8 %fusion.5 = f32[512,512]{0,1:T(8,128)S(1)} fusion(bf16[1,512,4096]{2,1,0:T(8,128)(2,1)} %param.6, bf16[4096,1024]{0,1:T(8,128)(2,1)} %constant_dynamic-update-slice_fusion, s32[]{:T(128)S(6)} %select_n.14), kind=kOutput, calls=%fused_computation.6 | convolution fusion | flops 2147483648 | bytes 9437188 | tf_op jit(solution)/shard_map/dot_general | solution.py:33
  326.3 29.9 %all-reduce.2 = bf16[512,512]{0,1:T(8,128)(2,1)S(1)} all-reduce(f32[512,512]{0,1:T(8,128)S(1)} %fusion.5), channel_id=1, replica_groups=mesh['dp'=4,'ctx'=2,'hidden'=4] {'hidden'}, use_global_device_ids=true, to_apply=%region_0.1 | all-reduce | flops 262144 | bytes 1572864 | tf_op jit(solution)/shard_map/psum | solution.py:39
  356.2 1.2 fusion.10
  357.5 12.4 %all-reduce.3 = bf16[512,128]{1,0:T(8,128)(2,1)S(1)} all-reduce(f32[512,128]{1,0:T(8,128)S(1)} %fusion.10), channel_id=1, replica_groups=mesh['dp'=4,'ctx'=2,'hidden'=4] {'ctx'}, use_global_device_ids=true, to_apply=%region_2.3 | all-reduce | flops 65536 | bytes 393216 | tf_op jit(solution)/shard_map/psum | solution.py:41
  369.8 0.2 convolution_bitcast_fusion
  370.1 0.8 copy.6
  (13 shorter events, 0.1 us)
Async XLA Ops:
  6.5 363.3 %copy-start = (bf16[256,512]{1,0:T(8,128)(2,1)S(1)}, bf16[256,512]{1,0:T(8,128)(2,1)}, u32[]{:S(2)}) copy-start(bf16[256,512]{1,0:T(8,128)(2,1)} %param.9) | copy-start | bytes 786436
  6.5 297.2 %all-gather.2.cloned.1.call-start = ((), (), s32[]{:S(2)}) async-start(), calls=%async_computation.1 | async-start | bytes 15335424 | tf_op jit(solution)/shard_map/all_gather | solution.py:30
  7.3 349.0 %reduce-scatter.2.cloned.1.call-start = ((), (), s32[]{:S(2)}) async-start(), calls=%async_computation.2 | async-start | bytes 1310720 | tf_op jit(solution)/shard_map/reduce_scatter | solution.py:36
  7.3 21.5 %collective-permute-start = (bf16[4096,64]{0,1:T(8,128)(2,1)}, bf16[4096,64]{0,1:T(8,128)(2,1)S(1)}, u32[]{:S(2)}, u32[]{:S(2)}) collective-permute-start(bf16[4096,64]{0,1:T(8,128)(2,1)} %param.8), channel_id=1, source_target_pairs={{0,28},{4,0},{8,4},{12,8},{16,12},{20,16},{24,20},{28,24},{1,29},{... | collective-permute-start | bytes 1572872 | tf_op jit(solution)/shard_map/ppermute | solution.py:12
  28.8 71.5 %copy-start.2 = (bf16[4096,64]{0,1:T(8,128)(2,1)}, bf16[4096,64]{0,1:T(8,128)(2,1)S(1)}, u32[]{:S(2)}) copy-start(bf16[4096,64]{0,1:T(8,128)(2,1)S(1)} %collective-permute-done) | copy-start | bytes 1572868
  30.1 70.2 %collective-permute-start.1 = (bf16[4096,128]{0,1:T(8,128)(2,1)S(1)}, bf16[4096,128]{0,1:T(8,128)(2,1)S(1)}, u32[]{:S(2)}, u32[]{:S(2)}) collective-permute-start(bf16[4096,128]{0,1:T(8,128)(2,1)S(1)} %pad_maximum_fusion.1), channel_id=1, source_target_pairs={{0,24},{4,28},{8,0},{12,4},{16,8},{20,12},{24,16},{28,20},{1,25},{... | collective-permute-start | bytes 3145736 | tf_op jit(solution)/shard_map/ppermute | solution.py:12
  102.9 175.7 %collective-permute-start.2 = (bf16[4096,256]{0,1:T(8,128)(2,1)}, bf16[4096,256]{0,1:T(8,128)(2,1)S(1)}, u32[]{:S(2)}, u32[]{:S(2)}) collective-permute-start(bf16[4096,256]{0,1:T(8,128)(2,1)} %pad_maximum_fusion), channel_id=1, source_target_pairs={{0,16},{4,20},{8,24},{12,28},{16,0},{20,4},{24,8},{28,12},{1,17},{... | collective-permute-start | bytes 6291464 | tf_op jit(solution)/shard_map/ppermute | solution.py:12
  102.9 177.2 %copy-start.1 = (bf16[4096,64]{0,1:T(8,128)(2,1)S(1)}, bf16[4096,64]{0,1:T(8,128)(2,1)}, u32[]{:S(2)}) copy-start(bf16[4096,64]{0,1:T(8,128)(2,1)} %param.8) | copy-start | bytes 1572868
  102.9 178.1 %copy-start.3 = (bf16[4096,64]{0,1:T(8,128)(2,1)S(1)}, bf16[4096,64]{0,1:T(8,128)(2,1)}, u32[]{:S(2)}) copy-start(bf16[4096,64]{0,1:T(8,128)(2,1)} %copy-done.2) | copy-start | bytes 1572868
Sparse Core Ops, SparseCore 0:
  9.5 294.1 all-gather.1
  319.0 28.3 reduce-scatter.1
